TPU v7x, 256 devices: a whole 4x4x8 slice. The times are simulated.
256 devices in a mesh: dp: 16 (over z, x_lo), ctx: 16 (over x_hi, y, core).
Axes of the slice: x: 4 (x_hi: 2, x_lo: 2; x = x_hi * 2 + x_lo), y: 4, z: 8, core: 2. Of those that a mesh axis runs over, the one named last changes fastest.
Arguments:
- normed: bfloat16 [16, 4096, 2048], P('dp', 'ctx'), may hold values from -21 to 21
- token_ids: int32 [16, 4096], P('dp', 'ctx'), may hold values from 0 to 128255
- block_order: int32 [16], replicated, may hold values from 0 to 15, each once
- master_weight: float32 [2048, 3072], P(('dp', 'ctx')), may hold values from -0.125 to 0.125
- weight_grad: float32 [2048, 3072], P(('dp', 'ctx')), may hold values from -6 to 6
- moment_one: float32 [2048, 3072], P(('dp', 'ctx')), may hold values from -4 to 4
- moment_two: float32 [2048, 3072], P(('dp', 'ctx')), may hold values from 0.1 to 3
Outputs:
- new_master: float32 [2048, 3072], P(('dp', 'ctx'))
- new_moment_one: float32 [2048, 3072], P(('dp', 'ctx'))
- new_moment_two: float32 [2048, 3072], P(('dp', 'ctx'))
- attended: bfloat16 [16, 4096, 2048], P('dp', 'ctx')
All inputs are finite; a program needn't handle non-finite values.
Results may differ from a plain program's by a relative error of at most 0.008.
The roundings to bfloat16 on the way count: a program that leaves them out, or rounds other values in their place, can miss the bound.
Values may be sent and summed in bfloat16 or wider, within the bound.
A program may use at most 64 MiB of HBM per device.

v0:
```python
import jax
import jax.numpy as jnp
from jax import lax
from jax.sharding import PartitionSpec as P

HQ = 16
HK = 4
DH = 128
GROUP = 4


beta_one = 0.9
beta_two = 0.95
adam_step = 10.0
learn_rate = 0.0003
decay_rate = 0.1
adam_eps = 1e-08
rope_theta = 500000.0
masked_score = -1e30


def passed_along(x, axis, by):
    count = lax.axis_size(axis)
    return lax.ppermute(x, axis, [(i, (i + by) % count) for i in range(count)])


def adam_update(master_weight, weight_grad, moment_one, moment_two):
    fresh_one = beta_one * moment_one + (1.0 - beta_one) * weight_grad
    fresh_two = beta_two * moment_two + (1.0 - beta_two) * weight_grad * weight_grad
    fix_one = 1.0 - beta_one**adam_step
    fix_two = 1.0 - beta_two**adam_step
    step_size = fresh_one / fix_one / (jnp.sqrt(fresh_two / fix_two) + adam_eps)
    fresh_master = master_weight - learn_rate * (step_size + decay_rate * master_weight)
    return (fresh_master, fresh_one, fresh_two)


def rotate(values, positions):
    half_dim = values.shape[-1] // 2
    frequency = rope_theta ** (-2.0 * jnp.arange(half_dim, dtype=jnp.float32) / values.shape[-1])
    angles = positions.astype(jnp.float32)[:, None] * frequency[None, :]
    cosine = jnp.cos(angles)[:, None, :]
    sine_part = jnp.sin(angles)[:, None, :]
    first_half = values[..., :half_dim]
    second_half = values[..., half_dim:]
    return jnp.concatenate(
        [
            first_half * cosine - second_half * sine_part,
            second_half * cosine + first_half * sine_part,
        ],
        -1,
    )


def local(normed, token_ids, block_order, master_weight, weight_grad, moment_one, moment_two):
    new_master, new_moment_one, new_moment_two = adam_update(
        master_weight, weight_grad, moment_one, moment_two
    )
    fresh_weight = new_master.astype(jnp.bfloat16)
    tok_rows = normed[0]
    block_len = tok_rows.shape[0]
    projected = jnp.dot(
        tok_rows,
        lax.all_gather(fresh_weight, ("dp", "ctx"), axis=0, tiled=True),
        preferred_element_type=jnp.float32,
    )
    place = lax.axis_index("ctx")
    place_count = lax.axis_size("ctx")
    local_idx = jnp.arange(block_len, dtype=jnp.int32)
    my_block = block_order[place]
    positions = my_block * block_len + local_idx
    doc_gap = block_len * place_count // 2
    marks = jnp.where(token_ids[0] % doc_gap == 0, positions, 0)
    last_mark = jnp.max(marks)
    all_marks = lax.all_gather(last_mark[None], "ctx", axis=0, tiled=True)
    prior_mark = jnp.max(jnp.where(block_order < my_block, all_marks, 0))
    doc_start = jnp.maximum(lax.cummax(marks, axis=0), prior_mark)
    queries = rotate(projected[:, : HQ * DH].reshape(block_len, HQ, DH), positions).astype(
        jnp.bfloat16
    )
    key_rows = rotate(
        projected[:, HQ * DH : (HQ + HK) * DH].reshape(block_len, HK, DH), positions
    ).astype(jnp.bfloat16)
    value_rows = projected[:, (HQ + HK) * DH :].astype(jnp.bfloat16)
    key_block = jnp.concatenate([key_rows.reshape(block_len, HK * DH), value_rows], 1)
    score_scale = DH ** (-0.5)

    def attend_head(carry, kv_head, key_part, value_part, key_pos):
        run_max, run_sum, run_acc = carry
        group_q = queries[:, kv_head * GROUP : (kv_head + 1) * GROUP, :]
        scores = (
            jnp.einsum("qjd,kd->jqk", group_q, key_part, preferred_element_type=jnp.float32)
            * score_scale
        )
        allowed = (key_pos[None, :] <= positions[:, None]) & (
            key_pos[None, :] >= doc_start[:, None]
        )
        scores = jnp.where(allowed[None], scores, masked_score)
        new_max = jnp.maximum(run_max, jnp.max(scores, -1))
        weights = jnp.where(allowed[None], jnp.exp(scores - new_max[..., None]), 0.0)
        factor = jnp.exp(run_max - new_max)
        run_sum = run_sum * factor + jnp.sum(weights, -1)
        run_acc = run_acc * factor[..., None] + jnp.einsum(
            "jqk,kd->jqd",
            weights.astype(jnp.bfloat16),
            value_part,
            preferred_element_type=jnp.float32,
        )
        return (new_max, run_sum, run_acc)

    def attend_block(carries, moving, source, head_list):
        key_pos = block_order[source] * block_len + local_idx
        head_count = len(head_list)
        updated = list(carries)
        for slot, kv_head in enumerate(head_list):
            key_part = moving[:, slot * DH : (slot + 1) * DH]
            value_part = moving[:, (head_count + slot) * DH : (head_count + slot + 1) * DH]
            updated[kv_head] = attend_head(carries[kv_head], kv_head, key_part, value_part, key_pos)
        return tuple(updated)

    start_state = (
        jnp.full((GROUP, block_len), masked_score, jnp.float32),
        jnp.zeros((GROUP, block_len), jnp.float32),
        jnp.zeros((GROUP, block_len, DH), jnp.float32),
    )
    carries = tuple((start_state for kv_head in range(HK)))
    every_head = list(range(HK))
    carries = attend_block(carries, key_block, place, every_head)

    def one_step(step_idx, state):
        held, moving = state
        moving = passed_along(moving, "ctx", 1)
        source = (place - step_idx - 1) % place_count
        return (attend_block(held, moving, source, every_head), moving)

    carries, unused_block = lax.fori_loop(0, place_count - 1, one_step, (carries, key_block))
    head_outputs = []
    for kv_head in range(HK):
        run_max, run_sum, run_acc = carries[kv_head]
        normalized = run_acc / run_sum[..., None]
        head_outputs.append(jnp.transpose(normalized, (1, 0, 2)).reshape(block_len, GROUP * DH))
    attended = jnp.concatenate(head_outputs, 1).astype(jnp.bfloat16)
    return (new_master, new_moment_one, new_moment_two, attended[None])


def solution(mesh):
    in_specs = (
        P("dp", "ctx", None),
        P("dp", "ctx"),
        P(),
        P(("dp", "ctx"), None),
        P(("dp", "ctx"), None),
        P(("dp", "ctx"), None),
        P(("dp", "ctx"), None),
    )
    out_specs = (
        P(("dp", "ctx"), None),
        P(("dp", "ctx"), None),
        P(("dp", "ctx"), None),
        P("dp", "ctx", None),
    )
    return jax.shard_map(local, mesh=mesh, in_specs=in_specs, out_specs=out_specs, check_vma=False)
```

profile of v0, /device:TPU:1, one launch (start us, length us, event | category | flops | bytes accessed | tf_op | source)
XLA Modules:
  0.0 749.4 jit_solution(6095916171341330654)
XLA Ops:
  7.2 1.9 fusion.107
  11.0 1.4 fusion.92
  16.0 1.4 dynamic-update-slice
  17.4 12.5 %all-reduce = s32[16]{0:T(128)S(1)} all-reduce(s32[16]{0:T(128)S(1)} %dynamic-update-slice), channel_id=1, replica_groups=mesh['dp'=16,'ctx'=16] {'ctx'}, use_global_device_ids=true, to_apply=%add | all-reduce | flops 16 | bytes 128
  30.0 2.0 fusion.94
  32.9 403.3 %all-gather.2.cloned.1.call-done = bf16[2048,3072]{1,0:T(8,128)(2,1)} async-done(((bf16[8,3072]{1,0:T(8,128)(2,1)}), bf16[2048,3072]{1,0:T(8,128)(2,1)}) %all-gather.2.cloned.1.call-update) | async-done | bytes 12582928 | tf_op jit(solution)/shard_map/all_gather | solution.py:63
  436.2 9.7 %fusion.118 = (bf16[256,3072]{0,1:T(8,128)(2,1)}, f32[256,3072]{0,1:T(8,128)S(1)}) fusion(bf16[2048,3072]{1,0:T(8,128)(2,1)} %all-gather.2.cloned.1.call-done, bf16[1,256,2048]{2,1,0:T(8,128)(2,1)S(1)} %copy-done), kind=kOutput, calls=%fused_computation.202 | convolution fusion | flops 3222011904 | bytes 18350080 | tf_op jit(solution)/shard_map/dot_general | solution.py:61
  446.9 1.5 fusion.113
  448.4 1.8 copy.110
  450.2 3.2 copy.111
  454.5 2.2 add_convert_fusion
  462.1 2.1 convolution_add_fusion.6
  464.2 2.1 convolution_add_fusion.5
  466.3 2.1 convolution_add_fusion.4
  469.5 268.7 %while.40 = (s32[]{:T(128)}, f32[4,256]{1,0:T(4,128)S(1)}, f32[4,256]{1,0:T(4,128)S(1)}, f32[4,256,128]{2,1,0:T(8,128)S(1)}, f32[4,256]{1,0:T(4,128)S(1)}, /*ind...) while((s32[]{:T(128)}, f32[4,256]{1,0:T(4,128)S(1)}, ...), condition=%wide.region_21.22_spmd.clone, body=%wide.region_12.21_spmd.clone.sunk | while | flops 547561984 | bytes 35001972 | solution.py:135
  470.8 5.1 collective-permute-done
  481.9 2.4 collective-permute-start
  485.7 7.0 collective-permute-done
  500.5 10.6 %collective-permute-done = bf16[256,1024]{1,0:T(8,128)(2,1)S(1)} collective-permute-done((bf16[256,1024]{1,0:T(8,128)(2,1)}, bf16[256,1024]{1,0:T(8,128)(2,1)S(1)}, u32[]{:S(2)}, u32[]{:S(2)}) %collective-permute-start) | collective-permute-done | bytes 524320 | tf_op jit(solution)/shard_map/while/body/eval_jaxpr/ppermute | solution.py:24
  518.4 11.1 %collective-permute-done = bf16[256,1024]{1,0:T(8,128)(2,1)S(1)} collective-permute-done((bf16[256,1024]{1,0:T(8,128)(2,1)}, bf16[256,1024]{1,0:T(8,128)(2,1)S(1)}, u32[]{:S(2)}, u32[]{:S(2)}) %collective-permute-start) | collective-permute-done | bytes 524320 | tf_op jit(solution)/shard_map/while/body/eval_jaxpr/ppermute | solution.py:24
  536.8 11.1 %collective-permute-done = bf16[256,1024]{1,0:T(8,128)(2,1)S(1)} collective-permute-done((bf16[256,1024]{1,0:T(8,128)(2,1)}, bf16[256,1024]{1,0:T(8,128)(2,1)S(1)}, u32[]{:S(2)}, u32[]{:S(2)}) %collective-permute-start) | collective-permute-done | bytes 524320 | tf_op jit(solution)/shard_map/while/body/eval_jaxpr/ppermute | solution.py:24
  555.3 11.1 %collective-permute-done = bf16[256,1024]{1,0:T(8,128)(2,1)S(1)} collective-permute-done((bf16[256,1024]{1,0:T(8,128)(2,1)}, bf16[256,1024]{1,0:T(8,128)(2,1)S(1)}, u32[]{:S(2)}, u32[]{:S(2)}) %collective-permute-start) | collective-permute-done | bytes 524320 | tf_op jit(solution)/shard_map/while/body/eval_jaxpr/ppermute | solution.py:24
  573.7 11.1 %collective-permute-done = bf16[256,1024]{1,0:T(8,128)(2,1)S(1)} collective-permute-done((bf16[256,1024]{1,0:T(8,128)(2,1)}, bf16[256,1024]{1,0:T(8,128)(2,1)S(1)}, u32[]{:S(2)}, u32[]{:S(2)}) %collective-permute-start) | collective-permute-done | bytes 524320 | tf_op jit(solution)/shard_map/while/body/eval_jaxpr/ppermute | solution.py:24
  592.1 11.1 %collective-permute-done = bf16[256,1024]{1,0:T(8,128)(2,1)S(1)} collective-permute-done((bf16[256,1024]{1,0:T(8,128)(2,1)}, bf16[256,1024]{1,0:T(8,128)(2,1)S(1)}, u32[]{:S(2)}, u32[]{:S(2)}) %collective-permute-start) | collective-permute-done | bytes 524320 | tf_op jit(solution)/shard_map/while/body/eval_jaxpr/ppermute | solution.py:24
  610.5 11.1 %collective-permute-done = bf16[256,1024]{1,0:T(8,128)(2,1)S(1)} collective-permute-done((bf16[256,1024]{1,0:T(8,128)(2,1)}, bf16[256,1024]{1,0:T(8,128)(2,1)S(1)}, u32[]{:S(2)}, u32[]{:S(2)}) %collective-permute-start) | collective-permute-done | bytes 524320 | tf_op jit(solution)/shard_map/while/body/eval_jaxpr/ppermute | solution.py:24
  629.0 11.1 %collective-permute-done = bf16[256,1024]{1,0:T(8,128)(2,1)S(1)} collective-permute-done((bf16[256,1024]{1,0:T(8,128)(2,1)}, bf16[256,1024]{1,0:T(8,128)(2,1)S(1)}, u32[]{:S(2)}, u32[]{:S(2)}) %collective-permute-start) | collective-permute-done | bytes 524320 | tf_op jit(solution)/shard_map/while/body/eval_jaxpr/ppermute | solution.py:24
  647.4 11.1 %collective-permute-done = bf16[256,1024]{1,0:T(8,128)(2,1)S(1)} collective-permute-done((bf16[256,1024]{1,0:T(8,128)(2,1)}, bf16[256,1024]{1,0:T(8,128)(2,1)S(1)}, u32[]{:S(2)}, u32[]{:S(2)}) %collective-permute-start) | collective-permute-done | bytes 524320 | tf_op jit(solution)/shard_map/while/body/eval_jaxpr/ppermute | solution.py:24
  665.8 11.1 %collective-permute-done = bf16[256,1024]{1,0:T(8,128)(2,1)S(1)} collective-permute-done((bf16[256,1024]{1,0:T(8,128)(2,1)}, bf16[256,1024]{1,0:T(8,128)(2,1)S(1)}, u32[]{:S(2)}, u32[]{:S(2)}) %collective-permute-start) | collective-permute-done | bytes 524320 | tf_op jit(solution)/shard_map/while/body/eval_jaxpr/ppermute | solution.py:24
  684.2 11.1 %collective-permute-done = bf16[256,1024]{1,0:T(8,128)(2,1)S(1)} collective-permute-done((bf16[256,1024]{1,0:T(8,128)(2,1)}, bf16[256,1024]{1,0:T(8,128)(2,1)S(1)}, u32[]{:S(2)}, u32[]{:S(2)}) %collective-permute-start) | collective-permute-done | bytes 524320 | tf_op jit(solution)/shard_map/while/body/eval_jaxpr/ppermute | solution.py:24
  702.7 11.1 %collective-permute-done = bf16[256,1024]{1,0:T(8,128)(2,1)S(1)} collective-permute-done((bf16[256,1024]{1,0:T(8,128)(2,1)}, bf16[256,1024]{1,0:T(8,128)(2,1)S(1)}, u32[]{:S(2)}, u32[]{:S(2)}) %collective-permute-start) | collective-permute-done | bytes 524320 | tf_op jit(solution)/shard_map/while/body/eval_jaxpr/ppermute | solution.py:24
  721.1 11.1 %collective-permute-done = bf16[256,1024]{1,0:T(8,128)(2,1)S(1)} collective-permute-done((bf16[256,1024]{1,0:T(8,128)(2,1)}, bf16[256,1024]{1,0:T(8,128)(2,1)S(1)}, u32[]{:S(2)}, u32[]{:S(2)}) %collective-permute-start) | collective-permute-done | bytes 524320 | tf_op jit(solution)/shard_map/while/body/eval_jaxpr/ppermute | solution.py:24
  738.1 1.3 fusion.88
  (613 shorter events, 116.1 us)
Async XLA Ops:
  7.2 429.0 %copy-start = (bf16[1,256,2048]{2,1,0:T(8,128)(2,1)S(1)}, bf16[1,256,2048]{2,1,0:T(8,128)(2,1)}, u32[]{:S(2)}) copy-start(bf16[1,256,2048]{2,1,0:T(8,128)(2,1)} %param.9) | copy-start | bytes 3145732
  7.2 429.0 %all-gather.2.cloned.1.call-start = ((), (), s32[]{:S(2)}) async-start(), calls=%async_computation | async-start | bytes 12632064 | tf_op jit(solution)/shard_map/all_gather | solution.py:63
  466.3 3.2 copy-start.9
  469.5 6.4 collective-permute-start
  478.0 1.4 copy-start.1
  481.9 10.7 %collective-permute-start = (bf16[256,1024]{1,0:T(8,128)(2,1)}, bf16[256,1024]{1,0:T(8,128)(2,1)S(1)}, u32[]{:S(2)}, u32[]{:S(2)}) collective-permute-start(bf16[256,1024]{1,0:T(8,128)(2,1)} %get-tuple-element.873), channel_id=1, source_target_pairs={{0,1},{1,2},{2,3},{3,4},{4,5},{5,6},{6,7},{7,8},{8,9},{9,10},{10,1... | collective-permute-start | bytes 1572872 | tf_op jit(solution)/shard_map/while/body/eval_jaxpr/ppermute | solution.py:24
  494.7 1.4 copy-start.1
  498.6 12.4 %collective-permute-start = (bf16[256,1024]{1,0:T(8,128)(2,1)}, bf16[256,1024]{1,0:T(8,128)(2,1)S(1)}, u32[]{:S(2)}, u32[]{:S(2)}) collective-permute-start(bf16[256,1024]{1,0:T(8,128)(2,1)} %get-tuple-element.873), channel_id=1, source_target_pairs={{0,1},{1,2},{2,3},{3,4},{4,5},{5,6},{6,7},{7,8},{8,9},{9,10},{10,1... | collective-permute-start | bytes 1572872 | tf_op jit(solution)/shard_map/while/body/eval_jaxpr/ppermute | solution.py:24
  513.1 1.4 copy-start.1
  517.0 12.4 %collective-permute-start = (bf16[256,1024]{1,0:T(8,128)(2,1)}, bf16[256,1024]{1,0:T(8,128)(2,1)S(1)}, u32[]{:S(2)}, u32[]{:S(2)}) collective-permute-start(bf16[256,1024]{1,0:T(8,128)(2,1)} %get-tuple-element.873), channel_id=1, source_target_pairs={{0,1},{1,2},{2,3},{3,4},{4,5},{5,6},{6,7},{7,8},{8,9},{9,10},{10,1... | collective-permute-start | bytes 1572872 | tf_op jit(solution)/shard_map/while/body/eval_jaxpr/ppermute | solution.py:24
  531.6 1.4 copy-start.1
  535.5 12.4 %collective-permute-start = (bf16[256,1024]{1,0:T(8,128)(2,1)}, bf16[256,1024]{1,0:T(8,128)(2,1)S(1)}, u32[]{:S(2)}, u32[]{:S(2)}) collective-permute-start(bf16[256,1024]{1,0:T(8,128)(2,1)} %get-tuple-element.873), channel_id=1, source_target_pairs={{0,1},{1,2},{2,3},{3,4},{4,5},{5,6},{6,7},{7,8},{8,9},{9,10},{10,1... | collective-permute-start | bytes 1572872 | tf_op jit(solution)/shard_map/while/body/eval_jaxpr/ppermute | solution.py:24
  550.0 1.4 copy-start.1
  553.9 12.4 %collective-permute-start = (bf16[256,1024]{1,0:T(8,128)(2,1)}, bf16[256,1024]{1,0:T(8,128)(2,1)S(1)}, u32[]{:S(2)}, u32[]{:S(2)}) collective-permute-start(bf16[256,1024]{1,0:T(8,128)(2,1)} %get-tuple-element.873), channel_id=1, source_target_pairs={{0,1},{1,2},{2,3},{3,4},{4,5},{5,6},{6,7},{7,8},{8,9},{9,10},{10,1... | collective-permute-start | bytes 1572872 | tf_op jit(solution)/shard_map/while/body/eval_jaxpr/ppermute | solution.py:24
  568.4 1.4 copy-start.1
  572.3 12.4 %collective-permute-start = (bf16[256,1024]{1,0:T(8,128)(2,1)}, bf16[256,1024]{1,0:T(8,128)(2,1)S(1)}, u32[]{:S(2)}, u32[]{:S(2)}) collective-permute-start(bf16[256,1024]{1,0:T(8,128)(2,1)} %get-tuple-element.873), channel_id=1, source_target_pairs={{0,1},{1,2},{2,3},{3,4},{4,5},{5,6},{6,7},{7,8},{8,9},{9,10},{10,1... | collective-permute-start | bytes 1572872 | tf_op jit(solution)/shard_map/while/body/eval_jaxpr/ppermute | solution.py:24
  586.8 1.4 copy-start.1
  590.7 12.4 %collective-permute-start = (bf16[256,1024]{1,0:T(8,128)(2,1)}, bf16[256,1024]{1,0:T(8,128)(2,1)S(1)}, u32[]{:S(2)}, u32[]{:S(2)}) collective-permute-start(bf16[256,1024]{1,0:T(8,128)(2,1)} %get-tuple-element.873), channel_id=1, source_target_pairs={{0,1},{1,2},{2,3},{3,4},{4,5},{5,6},{6,7},{7,8},{8,9},{9,10},{10,1... | collective-permute-start | bytes 1572872 | tf_op jit(solution)/shard_map/while/body/eval_jaxpr/ppermute | solution.py:24
  605.3 1.4 copy-start.1
  609.2 12.4 %collective-permute-start = (bf16[256,1024]{1,0:T(8,128)(2,1)}, bf16[256,1024]{1,0:T(8,128)(2,1)S(1)}, u32[]{:S(2)}, u32[]{:S(2)}) collective-permute-start(bf16[256,1024]{1,0:T(8,128)(2,1)} %get-tuple-element.873), channel_id=1, source_target_pairs={{0,1},{1,2},{2,3},{3,4},{4,5},{5,6},{6,7},{7,8},{8,9},{9,10},{10,1... | collective-permute-start | bytes 1572872 | tf_op jit(solution)/shard_map/while/body/eval_jaxpr/ppermute | solution.py:24
  627.6 12.4 %collective-permute-start = (bf16[256,1024]{1,0:T(8,128)(2,1)}, bf16[256,1024]{1,0:T(8,128)(2,1)S(1)}, u32[]{:S(2)}, u32[]{:S(2)}) collective-permute-start(bf16[256,1024]{1,0:T(8,128)(2,1)} %get-tuple-element.873), channel_id=1, source_target_pairs={{0,1},{1,2},{2,3},{3,4},{4,5},{5,6},{6,7},{7,8},{8,9},{9,10},{10,1... | collective-permute-start | bytes 1572872 | tf_op jit(solution)/shard_map/while/body/eval_jaxpr/ppermute | solution.py:24
  642.1 1.4 copy-start.1
  646.0 12.4 %collective-permute-start = (bf16[256,1024]{1,0:T(8,128)(2,1)}, bf16[256,1024]{1,0:T(8,128)(2,1)S(1)}, u32[]{:S(2)}, u32[]{:S(2)}) collective-permute-start(bf16[256,1024]{1,0:T(8,128)(2,1)} %get-tuple-element.873), channel_id=1, source_target_pairs={{0,1},{1,2},{2,3},{3,4},{4,5},{5,6},{6,7},{7,8},{8,9},{9,10},{10,1... | collective-permute-start | bytes 1572872 | tf_op jit(solution)/shard_map/while/body/eval_jaxpr/ppermute | solution.py:24
  660.5 1.4 copy-start.1
  664.4 12.4 %collective-permute-start = (bf16[256,1024]{1,0:T(8,128)(2,1)}, bf16[256,1024]{1,0:T(8,128)(2,1)S(1)}, u32[]{:S(2)}, u32[]{:S(2)}) collective-permute-start(bf16[256,1024]{1,0:T(8,128)(2,1)} %get-tuple-element.873), channel_id=1, source_target_pairs={{0,1},{1,2},{2,3},{3,4},{4,5},{5,6},{6,7},{7,8},{8,9},{9,10},{10,1... | collective-permute-start | bytes 1572872 | tf_op jit(solution)/shard_map/while/body/eval_jaxpr/ppermute | solution.py:24
  679.0 1.4 copy-start.1
  682.9 12.4 %collective-permute-start = (bf16[256,1024]{1,0:T(8,128)(2,1)}, bf16[256,1024]{1,0:T(8,128)(2,1)S(1)}, u32[]{:S(2)}, u32[]{:S(2)}) collective-permute-start(bf16[256,1024]{1,0:T(8,128)(2,1)} %get-tuple-element.873), channel_id=1, source_target_pairs={{0,1},{1,2},{2,3},{3,4},{4,5},{5,6},{6,7},{7,8},{8,9},{9,10},{10,1... | collective-permute-start | bytes 1572872 | tf_op jit(solution)/shard_map/while/body/eval_jaxpr/ppermute | solution.py:24
  697.4 1.4 copy-start.1
  701.3 12.4 %collective-permute-start = (bf16[256,1024]{1,0:T(8,128)(2,1)}, bf16[256,1024]{1,0:T(8,128)(2,1)S(1)}, u32[]{:S(2)}, u32[]{:S(2)}) collective-permute-start(bf16[256,1024]{1,0:T(8,128)(2,1)} %get-tuple-element.873), channel_id=1, source_target_pairs={{0,1},{1,2},{2,3},{3,4},{4,5},{5,6},{6,7},{7,8},{8,9},{9,10},{10,1... | collective-permute-start | bytes 1572872 | tf_op jit(solution)/shard_map/while/body/eval_jaxpr/ppermute | solution.py:24
  719.7 12.4 %collective-permute-start = (bf16[256,1024]{1,0:T(8,128)(2,1)}, bf16[256,1024]{1,0:T(8,128)(2,1)S(1)}, u32[]{:S(2)}, u32[]{:S(2)}) collective-permute-start(bf16[256,1024]{1,0:T(8,128)(2,1)} %get-tuple-element.873), channel_id=1, source_target_pairs={{0,1},{1,2},{2,3},{3,4},{4,5},{5,6},{6,7},{7,8},{8,9},{9,10},{10,1... | collective-permute-start | bytes 1572872 | tf_op jit(solution)/shard_map/while/body/eval_jaxpr/ppermute | solution.py:24
  738.1 1.7 copy-start.6
  738.1 2.2 copy-start.3
  (78 other events, 77.1 us)
Sparse Core Ops, SparseCore 0:
  10.4 425.6 all-gather.1
where the time goes:
time: 759 us; the launch traced here: 749 us
  waiting for transfers between devices  559 us (74%)
  matrix products  69 us (9%)
  local copies, waits for them, and re-layouts  49.7 us (7%)
  other arithmetic  29.4 us (4%)
  between operations  14.9 us (2%)
  blocking collectives  12.5 us (2%)
  loops' own time  12.3 us (2%)
    all_gather x1, waiting for transfers between devices, local(): lax.all_gather(fresh_weight, ('dp', 'ctx'), axis=0, tiled=True)  403 us
    ppermute x15, waiting for transfers between devices, passed_along(): return lax.ppermute(x, axis, [(i, (i + by) % count) for i in range(count)])  155 us
    dot_general x64, matrix products, attend_head(): jnp.einsum('jqk,kd->jqd', weights.astype(jnp.bfloat16), value_part, prefe...  38.2 us
    while x255, local copies, waits for them, and re-layouts  24.8 us
    dot_general x64, matrix products, attend_head(): jnp.einsum('qjd,kd->jqk', group_q, key_part, preferred_element_type=jnp.f...  21 us
  transfers between devices with their start and end apart: 16, of which 16 were waited for; matrix products, arithmetic and copies ran while one was open for 3% of the time, Pallas kernels for 0%

commit v1 on v0

v1 whole, which is shorter than its diff:
```python
import functools
import math

import jax
import jax.numpy as jnp
from jax import lax
from jax.experimental import pallas as pl
from jax.experimental.pallas import tpu as pltpu
from jax.sharding import PartitionSpec as P

HQ = 16
HK = 4
DH = 128
GROUP = 4
BLK = 256
D = 2048

beta_one = 0.9
beta_two = 0.95
adam_step = 10.0
learn_rate = 0.0003
decay_rate = 0.1
adam_eps = 1e-08
rope_theta = 500000.0
masked_score = -1e30
MESH = pl.DeviceIdType.MESH
LOG_SCALE = DH**-0.5 * math.log2(math.e)


def adam_update(master_weight, weight_grad, moment_one, moment_two):
    fresh_one = beta_one * moment_one + (1.0 - beta_one) * weight_grad
    fresh_two = beta_two * moment_two + (1.0 - beta_two) * weight_grad * weight_grad
    fix_one = 1.0 - beta_one**adam_step
    fix_two = 1.0 - beta_two**adam_step
    step_size = fresh_one / fix_one / (jnp.sqrt(fresh_two / fix_two) + adam_eps)
    fresh_master = master_weight - learn_rate * (step_size + decay_rate * master_weight)
    return (fresh_master, fresh_one, fresh_two)


class Place:
    def __init__(self):
        dp = lax.axis_index("dp")
        ctx = lax.axis_index("ctx")
        self.z, x_lo = dp // 2, dp % 2
        x_hi = ctx // 8
        self.y = (ctx // 2) % 4
        self.core = ctx % 2
        self.x = x_hi * 2 + x_lo

    def at(self, x=None, y=None, z=None, core=None):
        x = self.x if x is None else x
        y = self.y if y is None else y
        z = self.z if z is None else z
        core = self.core if core is None else core
        return (z * 2 + x % 2, (x // 2) * 8 + y * 2 + core)


class Sender:
    def __init__(self, send_sem, recv_sem):
        self.send_sem, self.recv_sem, self.started = send_sem, recv_sem, []

    def __call__(self, src, dst, device):
        n = len(self.started)
        copy = pltpu.make_async_remote_copy(
            src_ref=src,
            dst_ref=dst,
            send_sem=self.send_sem.at[n],
            recv_sem=self.recv_sem.at[n],
            device_id=device,
            device_id_type=MESH,
        )
        copy.start()
        self.started.append(copy)
        return copy

    def drain(self):
        for copy in self.started:
            copy.wait_send()


def greet(devices):
    barrier = pltpu.get_barrier_semaphore()
    for device in devices:
        pl.semaphore_signal(barrier, inc=1, device_id=device, device_id_type=MESH)
    pl.semaphore_wait(barrier, len(devices))


def ring(send, n, p, block, half, device):
    right, left = device((p + 1) % n), device((p + n - 1) % n)
    to_right = send(block(p), block(p), right)
    to_left = send(block(p), block(p), left)
    yield
    for step in range(1, n // 2):
        from_left, from_right = (p + n - step) % n, (p + step) % n
        piece = block if step < n // 2 - 1 else None
        to_right.wait_recv()
        src = piece(from_left) if piece else half(from_left, 0)
        to_right = send(src, src, right)
        to_left.wait_recv()
        src = piece(from_right) if piece else half(from_right, 1)
        to_left = send(src, src, left)
        yield
    to_right.wait_recv()
    to_left.wait_recv()


def gather_kernel(
    x_ref, w_ref, lm_ref, mark_ref, before_ref, cos_ref, sin_ref,
    q_ref, kv_ref, ds_ref,
    wbuf, x2, lm2, mk, send_sem, recv_sem, own_sem,
):
    me = Place()
    x, y, z, core = me.x, me.y, me.z, me.core
    xs = (x % 2) * 2 + x // 2
    other = 1 - core
    partner = me.at(core=other)

    def slot(xv):
        return (xv % 2) * 2 + xv // 2

    rows = pl.ds(pl.multiple_of(core * 8, 8), 8)
    own = [
        pltpu.make_async_copy(w_ref.at[core], wbuf.at[:, z, xs, y, rows, :], own_sem.at[0]),
        pltpu.make_async_copy(x_ref, x2.at[core], own_sem.at[1]),
        pltpu.make_async_copy(lm_ref, lm2.at[core], own_sem.at[2]),
        pltpu.make_async_copy(mark_ref, mk.at[xs, y, core], own_sem.at[3]),
    ]
    for copy in own:
        copy.start()
    greet(
        [partner]
        + [me.at(x=(x + d) % 4) for d in (1, 3)]
        + [me.at(y=(y + d) % 4) for d in (1, 3)]
        + [me.at(z=(z + d) % 8) for d in (1, 7)]
    )
    send = Sender(send_sem, recv_sem)
    w_there = send(w_ref.at[other], wbuf.at[:, z, xs, y, rows, :], partner)
    mark_there = send(mark_ref, mk.at[xs, y, core], partner)
    x_there = send(x_ref, x2.at[core], partner)
    lm_there = send(lm_ref, lm2.at[core], partner)
    own[0].wait()
    own[3].wait()
    w_there.wait_recv()
    mark_there.wait_recv()

    def by_x(xv):
        return me.at(x=xv)

    def by_y(yv):
        return me.at(y=yv)

    def by_z(zv):
        return me.at(z=zv)

    cols = (pl.ds(0, 256), pl.ds(256, 256))

    def color_zero():
        w = wbuf.at[0]
        yield from ring(send, 4, x, lambda v: w.at[z, slot(v), y], lambda v, h: w.at[z, slot(v), y, :, cols[h]], by_x)
        yield from ring(send, 4, y, lambda v: w.at[z, :, v], lambda v, h: w.at[z, pl.ds(2 * h, 2), v], by_y)
        yield from ring(send, 8, z, lambda v: w.at[v], lambda v, h: w.at[v, pl.ds(2 * h, 2)], by_z)

    def color_one():
        w = wbuf.at[1]
        yield from ring(send, 4, y, lambda v: w.at[z, xs, v], lambda v, h: w.at[z, xs, v, :, cols[h]], by_y)
        yield from ring(send, 8, z, lambda v: w.at[v, xs], lambda v, h: w.at[v, xs, pl.ds(2 * h, 2)], by_z)
        yield from ring(send, 4, x, lambda v: w.at[:, slot(v)], lambda v, h: w.at[pl.ds(4 * h, 4), slot(v)], by_x)

    def color_two():
        w = wbuf.at[2]
        yield from ring(send, 8, z, lambda v: w.at[v, xs, y], lambda v, h: w.at[v, xs, y, :, cols[h]], by_z)
        yield from ring(send, 4, x, lambda v: w.at[:, slot(v), y], lambda v, h: w.at[pl.ds(4 * h, 4), slot(v), y], by_x)
        yield from ring(send, 4, y, lambda v: w.at[:, :, v], lambda v, h: w.at[pl.ds(4 * h, 4), :, v], by_y)

    def marks():
        yield from ring(send, 4, y, lambda v: mk.at[xs, v], lambda v, h: mk.at[xs, v, pl.ds(h, 1)], by_y)
        yield from ring(send, 4, x, lambda v: mk.at[slot(v)], lambda v, h: mk.at[slot(v), pl.ds(2 * h, 2)], by_x)

    chains = [color_zero(), color_one(), color_two(), marks()]

    def project(color):
        rows_in = x2[...].reshape(2 * BLK, D)
        return jnp.dot(rows_in, wbuf[color].reshape(D, 512), preferred_element_type=jnp.float32)

    def rotated(part):
        turned = pltpu.roll(part, DH // 2, 1)
        return (part * cos_ref[...] + turned * sin_ref[...]).astype(jnp.bfloat16)

    def queries(color):
        out = project(color)
        for h in range(4):
            q_ref[color * 4 + h] = rotated(out[:, h * DH : (h + 1) * DH])

    order = [0, 1, 2, 3] * 4 + [0, 1, 2, 3] + [1, 2, 1, 2, 0, 0, 1, 2, 0]
    for chain in order:
        next(chains[chain], None)
    own[1].wait()
    own[2].wait()
    x_there.wait_recv()
    lm_there.wait_recv()
    x_lo = x % 2
    heard = mk[pl.ds(x_lo * 2, 2)].reshape(16, 8, 128)
    for b in range(2):
        prior = jnp.max(heard * before_ref[b], axis=0)
        ds_ref[b * BLK : (b + 1) * BLK, :] = jnp.maximum(lm2[b], prior[0:1, :])
    for _ in chains[0]:
        pass
    queries(0)
    for _ in chains[1]:
        pass
    queries(1)
    for _ in chains[2]:
        pass
    for _ in chains[3]:
        pass
    out = project(2)
    for g in range(2):
        kv_ref[g, :, :DH] = rotated(out[:, g * 256 : g * 256 + DH])
        kv_ref[g, :, DH:] = out[:, g * 256 + DH : (g + 1) * 256].astype(jnp.bfloat16)
    send.drain()


def attend_kernel(
    q_ref, kv_ref, ds_ref, qpos_ref, kpos_ref,
    out_ref,
    kvbuf, relay_a, relay_b, m_ref, l_ref, acc_ref, bias_ref, ostage,
    send_sem, recv_sem, own_sem,
):
    me = Place()
    x, y, core = me.x, me.y, me.core
    xh = x // 2
    far = 1 - xh
    other = 1 - core
    partner = me.at(core=other)
    own = pltpu.make_async_copy(kv_ref, kvbuf.at[:, xh, y], own_sem)
    own.start()
    right_x, left_x = me.at(x=(x + 1) % 4), me.at(x=(x + 3) % 4)
    right_y, left_y = me.at(y=(y + 1) % 4), me.at(y=(y + 3) % 4)
    greet([partner, right_x, left_x, right_y, left_y])
    send = Sender(send_sem, recv_sem)
    lo, hi = pl.ds(0, BLK), pl.ds(BLK, BLK)
    y_r, y_l, y_f = (y + 1) % 4, (y + 3) % 4, (y + 2) % 4
    from_left_x, from_right_x = ((x + 3) % 4) // 2, ((x + 1) % 4) // 2

    def first_leg(src, relay):
        return send(src.at[lo], relay(0), right_x), send(src.at[hi], relay(1), left_x)

    def second_leg(legs, relay, head, yv):
        legs[0].wait_recv()
        one = send(relay(0), kvbuf.at[head, from_left_x, yv, lo], right_x)
        legs[1].wait_recv()
        two = send(relay(1), kvbuf.at[head, from_right_x, yv, hi], left_x)
        return one, two

    def landed(pair):
        for copy in pair:
            copy.wait_recv()

    def rel_a(d):
        return relay_a.at[d]

    def rel_b(k):
        return lambda d: relay_b.at[d, k]

    def piece(head, xv, yv, first=False):
        chip = xv * 4 + yv
        kpos = kpos_ref[chip][0:1, :]
        for r in range(4):
            part = slice(r * 128, (r + 1) * 128)
            qpos = qpos_ref[part, 0:1]
            start = ds_ref[part, 0:1]
            allowed = (kpos <= qpos) & (kpos >= start)
            bias_ref[part, :] = jnp.where(allowed, 0.0, masked_score)

        def one_head(j, carry):
            h = head * GROUP + j
            keys = kvbuf[head, xv, yv, :, :DH]
            values = kvbuf[head, xv, yv, :, DH:]

            def raw(r):
                return lax.dot_general(
                    q_ref[h, r * 128 : (r + 1) * 128, :], keys, (((1,), (1,)), ((), ())),
                    preferred_element_type=jnp.float32,
                )

            ahead = raw(0)
            for r in range(4):
                part = slice(r * 128, (r + 1) * 128)
                s = ahead * LOG_SCALE + bias_ref[part, :]
                if r < 3:
                    ahead = raw(r + 1)
                top = jnp.broadcast_to(jnp.max(s, axis=1, keepdims=True), (128, 128))
                if not first:
                    old = m_ref[h, part, :]
                    top = jnp.maximum(old, top)
                    fade = jnp.exp2(old - top)
                m_ref[h, part, :] = top
                p = jnp.exp2(s - jnp.tile(top, (1, 4)))
                total = p[:, 0:128] + p[:, 128:256] + p[:, 256:384] + p[:, 384:512]
                pv = jnp.dot(p.astype(jnp.bfloat16), values, preferred_element_type=jnp.float32)
                if first:
                    l_ref[h, part, :] = total
                    acc_ref[h, part, :] = pv
                else:
                    l_ref[h, part, :] = l_ref[h, part, :] * fade + total
                    acc_ref[h, part, :] = acc_ref[h, part, :] * fade + pv
            return carry

        lax.fori_loop(0, GROUP, one_head, 0)

    def finish(head):
        rows_there = pl.ds(pl.multiple_of(other * BLK, BLK), BLK)
        rows_here = pl.ds(pl.multiple_of(core * BLK, BLK), BLK)
        for j in range(GROUP):
            h = head * GROUP + j
            under = jnp.sum(l_ref[h, rows_there, :], axis=1, keepdims=True)
            ostage[head, :, j * DH : (j + 1) * DH] = (acc_ref[h, rows_there, :] / under).astype(jnp.bfloat16)
        for j in range(GROUP):
            h = head * GROUP + j
            under = jnp.sum(l_ref[h, rows_here, :], axis=1, keepdims=True)
            at = pl.ds(pl.multiple_of(core * (8 * DH) + h * DH, DH), DH)
            out_ref[:, at] = (acc_ref[h, rows_here, :] / under).astype(jnp.bfloat16)
        at = pl.ds(pl.multiple_of(core * (8 * DH) + head * GROUP * DH, GROUP * DH), GROUP * DH)
        return send(ostage.at[head], out_ref.at[:, at], partner)

    a_x = first_leg(kv_ref.at[0], rel_a)
    b_y = (send(kv_ref.at[1], kvbuf.at[1, xh, y], right_y), send(kv_ref.at[1], kvbuf.at[1, xh, y], left_y))
    b_x0 = first_leg(kv_ref.at[1], rel_b(0))
    own.wait()
    piece(1, xh, y, True)
    a_far = second_leg(a_x, rel_a, 0, y)
    piece(0, xh, y, True)
    landed(b_y)
    b_f = (
        send(kvbuf.at[1, xh, y_l, lo], kvbuf.at[1, xh, y_l, lo], right_y),
        send(kvbuf.at[1, xh, y_r, hi], kvbuf.at[1, xh, y_r, hi], left_y),
    )
    b_x1 = first_leg(kvbuf.at[1, xh, y_l], rel_b(1))
    b_x2 = first_leg(kvbuf.at[1, xh, y_r], rel_b(2))
    piece(1, xh, y_l)
    landed(a_far)
    a_y = (
        send(kvbuf.at[0, :, y], kvbuf.at[0, :, y], right_y),
        send(kvbuf.at[0, :, y], kvbuf.at[0, :, y], left_y),
    )
    b_far0 = second_leg(b_x0, rel_b(0), 1, y)
    piece(1, xh, y_r)
    landed(b_f)
    b_x3 = first_leg(kvbuf.at[1, xh, y_f], rel_b(3))
    piece(0, far, y)
    b_far1 = second_leg(b_x1, rel_b(1), 1, y_l)
    piece(1, xh, y_f)
    landed(b_far0)
    b_far2 = second_leg(b_x2, rel_b(2), 1, y_r)
    piece(1, far, y)
    landed(a_y)
    a_f = (
        send(kvbuf.at[0, :, y_l, lo], kvbuf.at[0, :, y_l, lo], right_y),
        send(kvbuf.at[0, :, y_r, hi], kvbuf.at[0, :, y_r, hi], left_y),
    )
    b_far3 = second_leg(b_x3, rel_b(3), 1, y_f)
    piece(0, xh, y_l)
    piece(0, far, y_l)
    piece(0, xh, y_r)
    piece(0, far, y_r)
    landed(b_far1)
    piece(1, far, y_l)
    landed(b_far2)
    piece(1, far, y_r)
    landed(a_f)
    piece(0, xh, y_f)
    piece(0, far, y_f)
    done_a = finish(0)
    landed(b_far3)
    piece(1, far, y_f)
    done_b = finish(1)
    landed((done_a, done_b))
    send.drain()


VMEM = pl.BlockSpec(memory_space=pltpu.VMEM)


def local(normed, token_ids, block_order, master_weight, weight_grad, moment_one, moment_two):
    new_master, new_moment_one, new_moment_two = adam_update(
        master_weight, weight_grad, moment_one, moment_two
    )
    fresh = new_master.astype(jnp.bfloat16)
    halves = []
    for c in range(2):
        k0, v0 = 2048 + 256 * c, 2560 + 256 * c
        joined = jnp.concatenate(
            [fresh[:, k0 : k0 + 128], fresh[:, v0 : v0 + 128], fresh[:, k0 + 128 : k0 + 256], fresh[:, v0 + 128 : v0 + 256]], 1
        )
        halves.append(jnp.stack([fresh[:, 1024 * c : 1024 * c + 512], fresh[:, 1024 * c + 512 : 1024 * c + 1024], joined]))
    w_own = jnp.stack(halves)

    ctx = lax.axis_index("ctx")
    local_idx = jnp.arange(BLK, dtype=jnp.int32)
    my_block = block_order[ctx]
    positions = my_block * BLK + local_idx
    doc_gap = BLK * 16 // 2
    marks = jnp.where(token_ids[0] % doc_gap == 0, positions, 0)
    running = lax.cummax(marks, axis=0)
    lm = jnp.broadcast_to(running[:, None], (BLK, 128))
    mark_tile = jnp.broadcast_to(jnp.max(marks), (8, 128))
    pair = lax.dynamic_slice_in_dim(block_order, ctx - ctx % 2, 2)
    before = jnp.broadcast_to(
        (block_order[None, :] < pair[:, None]).astype(jnp.int32)[:, :, None, None], (2, 16, 8, 128)
    )
    pair_pos = (pair[:, None] * BLK + local_idx[None, :]).reshape(2 * BLK)
    half = DH // 2
    frequency = rope_theta ** (-2.0 * jnp.arange(half, dtype=jnp.float32) / DH)
    angles = pair_pos.astype(jnp.float32)[:, None] * frequency[None, :]
    cosine, sine = jnp.cos(angles), jnp.sin(angles)
    cos_full = jnp.concatenate([cosine, cosine], 1)
    sin_full = jnp.concatenate([-sine, sine], 1)
    qpos = jnp.broadcast_to(pair_pos[:, None], (2 * BLK, 128))
    kpos = (block_order[:, None] * BLK + local_idx[None, :]).reshape(8, 1, 2 * BLK)
    kpos = jnp.broadcast_to(kpos, (8, 8, 2 * BLK))

    q, kv, ds = pl.pallas_call(
        gather_kernel,
        out_shape=(
            jax.ShapeDtypeStruct((8, 2 * BLK, DH), jnp.bfloat16),
            jax.ShapeDtypeStruct((2, 2 * BLK, 2 * DH), jnp.bfloat16),
            jax.ShapeDtypeStruct((2 * BLK, 128), jnp.int32),
        ),
        in_specs=[VMEM] * 7,
        out_specs=[VMEM] * 3,
        scratch_shapes=[
            pltpu.VMEM((3, 8, 4, 4, 16, 512), jnp.bfloat16),
            pltpu.VMEM((2, BLK, D), jnp.bfloat16),
            pltpu.VMEM((2, BLK, 128), jnp.int32),
            pltpu.VMEM((4, 4, 2, 8, 128), jnp.int32),
            pltpu.SemaphoreType.DMA((64,)),
            pltpu.SemaphoreType.DMA((64,)),
            pltpu.SemaphoreType.DMA((4,)),
        ],
        compiler_params=pltpu.CompilerParams(
            collective_id=0, has_side_effects=True, vmem_limit_bytes=40 << 20
        ),
        name="gather_project",
    )(normed[0], w_own, lm, mark_tile, before, cos_full, sin_full)

    attended = pl.pallas_call(
        attend_kernel,
        out_shape=jax.ShapeDtypeStruct((BLK, HQ * DH), jnp.bfloat16),
        in_specs=[VMEM] * 5,
        out_specs=VMEM,
        scratch_shapes=[
            pltpu.VMEM((2, 2, 4, 2 * BLK, 2 * DH), jnp.bfloat16),
            pltpu.VMEM((2, BLK, 2 * DH), jnp.bfloat16),
            pltpu.VMEM((2, 4, BLK, 2 * DH), jnp.bfloat16),
            pltpu.VMEM((8, 2 * BLK, 128), jnp.float32),
            pltpu.VMEM((8, 2 * BLK, 128), jnp.float32),
            pltpu.VMEM((8, 2 * BLK, DH), jnp.float32),
            pltpu.VMEM((2 * BLK, 2 * BLK), jnp.float32),
            pltpu.VMEM((2, BLK, GROUP * DH), jnp.bfloat16),
            pltpu.SemaphoreType.DMA((32,)),
            pltpu.SemaphoreType.DMA((32,)),
            pltpu.SemaphoreType.DMA,
        ],
        compiler_params=pltpu.CompilerParams(
            collective_id=1, has_side_effects=True, vmem_limit_bytes=40 << 20
        ),
        name="attend",
    )(q, kv, ds, qpos, kpos)
    return (new_master, new_moment_one, new_moment_two, attended[None])


def solution(mesh):
    in_specs = (
        P("dp", "ctx", None),
        P("dp", "ctx"),
        P(),
        P(("dp", "ctx"), None),
        P(("dp", "ctx"), None),
        P(("dp", "ctx"), None),
        P(("dp", "ctx"), None),
    )
    out_specs = (
        P(("dp", "ctx"), None),
        P(("dp", "ctx"), None),
        P(("dp", "ctx"), None),
        P("dp", "ctx", None),
    )
    return jax.shard_map(local, mesh=mesh, in_specs=in_specs, out_specs=out_specs, check_vma=False)
```

time: 759 us -> 131 us (0.17); the launches traced: 749 us -> 131 us
  waiting for transfers between devices: 559 us -> 0 us
  Pallas kernels: 0 us -> 121 us
  matrix products: 69 us -> 0 us
  local copies, waits for them, and re-layouts: 49.7 us -> 5.2 us
  other arithmetic: 29.4 us -> 3.22 us
  between operations: 14.9 us -> 1.47 us
  blocking collectives: 12.5 us -> 0 us
  loops' own time: 12.3 us -> 0 us
    all_gather x1 -> x0, waiting for transfers between devices: 403 us -> none  [local(): lax.all_gather(fresh_weight, ('dp', 'ctx'), axis=0, tiled=True)]
    ppermute x15 -> x0, waiting for transfers between devices: 155 us -> none  [passed_along(): return lax.ppermute(x, axis, [(i, (i + by) % count) for i in range(count)])]
    pallas_call x0 -> x2, Pallas kernels: none -> 121 us  [the longest x1 66.5 us: local(): pl.pallas_call(attend_kernel, out_shape=jax.ShapeDtypeStruct((BLK, HQ * D...]
    dot_general x129 -> x0, matrix products: 69 us -> none  [the longest x64 38.2 us: attend_head(): jnp.einsum('jqk,kd->jqd', weights.astype(jnp.bfloat16), value_part, prefe...]
    while x255 -> x0, local copies, waits for them, and re-layouts: 24.8 us -> none
    unnamed x1 -> x0, blocking collectives: 12.5 us -> none
    another operation x1 -> x0, loops' own time: 12.3 us -> none  [local(): lax.fori_loop(0, place_count - 1, one_step, (carries, key_block))]
    reduce_sum x16 -> x0, other arithmetic: 12.1 us -> none  [attend_head(): run_sum = run_sum * factor + jnp.sum(weights, -1)]
  transfers between devices with their start and end apart: 16 -> 0, of which waited for: 16 -> 0; matrix products, arithmetic and copies ran while one was open for 3% -> 0% of each run, Pallas kernels for 0% -> 0%
where the time goes in v1:
time: 131 us
  Pallas kernels  121 us (92%)
  local copies, waits for them, and re-layouts  5.2 us (4%)
  other arithmetic  3.22 us (2%)
  between operations  1.47 us (1%)
    pallas_call x1, Pallas kernels, local(): pl.pallas_call(attend_kernel, out_shape=jax.ShapeDtypeStruct((BLK, HQ * D...  66.5 us
    pallas_call x1, Pallas kernels, local(): pl.pallas_call(gather_kernel, out_shape=(jax.ShapeDtypeStruct((8, 2 * BLK...  54.2 us
    unnamed x19, local copies, waits for them, and re-layouts  3.22 us

profile of v1, /device:TPU:1, one launch (start us, length us, event | category | flops | bytes accessed | tf_op | source)
XLA Modules:
  0.0 130.6 jit_solution(10375342812755890966)
XLA Ops:
  0.7 0.6 copy-done.6
  1.3 0.6 dynamic_slice.6
  2.5 0.0 copy-start.5
  2.5 0.7 copy-done.5
  3.2 0.6 fusion.4
  3.9 0.3 reduce-window.9
  4.2 0.1 broadcast_multiply_fusion.1
  4.3 0.1 compare_convert_fusion
  4.3 0.1 slice.55
  4.5 0.1 slice_reduce_fusion
  4.6 0.1 maximum_bitcast_fusion.4
  4.6 0.1 broadcast_bitcast_fusion
  4.7 0.1 add.115
  4.8 0.1 copy.12
  4.9 0.7 broadcast_in_dim.15.mark_ref
  5.6 0.1 add.116
  5.7 0.1 broadcast_in_dim.14.lm_ref
  5.8 0.0 copy-start.3
  5.8 0.0 copy-start.4
  5.8 0.1 broadcast_in_dim.16.before_ref
  5.9 0.1 broadcast_in_dim.17.qpos_ref
  6.0 0.6 copy-done.3
  6.7 0.0 copy-done.4
  6.7 0.1 copy-done.1
  6.8 0.0 copy-done.2
  6.8 0.7 fusion.6
  7.7 1.0 fusion.1
  8.7 0.2 pad_maximum_fusion
  8.9 0.0 copy-done
  8.9 54.2 %gather_project.1 = (bf16[8,512,128]{2,1,0:T(8,128)(2,1)S(1)}, bf16[2,512,256]{2,1,0:T(8,128)(2,1)S(1)}, s32[512,128]{1,0:T(8,128)S(1)}) custom-call(bf16[256,2048]{1,0:T(8,128)(2,1)S(1)} %bitcast.31, bf16[2,3,8,512]{3,2,1,0:T(8,128)(2,1)S(1)} %pad_maximum_fusion.2.w_ref, s32[256,128]{1,0:T(8,128)S(1)} %broadcast_in_dim.14.lm_ref, ...), custom_call_target="tpu_custom_call" | custom-call | tf_op jit(solution)/shard_map/gather_project/pallas_call | solution.py:422
  63.1 66.5 %attend.1 = bf16[256,2048]{1,0:T(8,128)(2,1)S(1)} custom-call(bf16[8,512,128]{2,1,0:T(8,128)(2,1)S(1)} %get-tuple-element.7.q_ref, bf16[2,512,256]{2,1,0:T(8,128)(2,1)S(1)} %get-tuple-element.8.kv_ref, s32[512,128]{1,0:T(8,128)S(1)} %get-tuple-element.9.ds_ref, s32[512,128]{1,0:T(8,128)S(1)} %broadcast_in_dim.17.qpos_ref, ...), custom_call_target="tpu_custom_call" | custom-call | tf_op jit(solution)/shard_map/attend/pallas_call | solution.py:446
  129.6 1.0 copy.16
  (20 shorter events, 0.2 us)
Async XLA Ops:
  0.6 0.7 copy-start.6
  2.5 0.7 copy-start.5
  5.8 0.9 copy-start.3
  5.8 0.9 copy-start.4
  5.9 0.9 copy-start.1
  5.9 1.0 copy-start.2
  7.7 1.2 copy-start
